TPU v7x, 256 devices: a whole 4x4x8 slice. The times are simulated.
256 devices in a mesh: out: 128 (over z, y, x), con: 2 (over core).
Axes of the slice: x: 4, y: 4, z: 8, core: 2. Of those that a mesh axis runs over, the one named last changes fastest.
Arguments:
- amplitudes: bfloat16 [512, 9216], P(('out', 'con')), may hold values from -6 to 6
- integrals: bfloat16 [131072, 9216], P('out', 'con'), may hold values from -0.078125 to 0.078125
- block_sizes: int32 [8], replicated, may hold values from 64 to 192, as said below
Outputs:
- ladder: bfloat16 [512, 131072], P('con', 'out')
Inputs may be any that keep to these rules, and one draw needn't show every extreme that they name: `block_sizes`: each entry lies between 64 and 192; the entries sum to 1024; one entry equals 192 and one equals 64.
All inputs are finite; a program needn't handle non-finite values.
Results may differ from a plain program's by a relative error of at most 0.001.
Values may be sent and summed in bfloat16 or wider, within the bound.
A program may use at most 64 MiB of HBM per device.

v0:
```python
import jax
import jax.numpy as jnp
from jax import lax
from jax.sharding import Mesh, PartitionSpec as P

DMAX = 192
TORUS = {128: (("z", 8), ("y", 4), ("x", 4))}


def mask_slots(amplitudes, block_sizes):
    row_count = amplitudes.shape[0]
    nirrep = block_sizes.shape[0]
    blocked = amplitudes.reshape(row_count, nirrep, -1, DMAX)
    valid_cols = jnp.arange(DMAX, dtype=jnp.int32)[None, :] < block_sizes[:, None]
    masked = jnp.where(valid_cols[None, :, None, :], blocked, jnp.zeros((), amplitudes.dtype))
    return masked.reshape(row_count, -1)


def contract(amp_rows, integrals):
    return lax.dot_general(
        amp_rows, integrals, (((1,), (1,)), ((), ())), preferred_element_type=jnp.float32
    )


def make_on_device(out_axes):

    def on_device(amplitudes, integrals, block_sizes):
        masked = mask_slots(amplitudes, block_sizes)
        con = lax.axis_index("con")
        con_count = lax.axis_size("con")
        half = integrals.shape[1]
        chip_rows = lax.all_gather(masked, "con", axis=0, tiled=True)
        all_rows = lax.dynamic_slice_in_dim(chip_rows, con * half, half, axis=1)
        for name in reversed(out_axes):
            all_rows = lax.all_gather(all_rows, name, axis=0, tiled=True)
        out_rows = all_rows.shape[0] // con_count
        other = 1 - con
        other_part = contract(
            lax.dynamic_slice_in_dim(all_rows, other * out_rows, out_rows, axis=0), integrals
        )
        received = lax.ppermute(other_part, "con", perm=[(0, 1), (1, 0)])
        own_part = contract(
            lax.dynamic_slice_in_dim(all_rows, con * out_rows, out_rows, axis=0), integrals
        )
        own_part = lax.optimization_barrier(own_part)
        return (own_part + received).astype(jnp.bfloat16)

    return on_device


def solution(mesh):
    n_out = mesh.shape["out"]
    axes = TORUS.get(n_out, (("out", n_out),))
    names = tuple((name for name, _ in axes))
    devices = mesh.devices.reshape(tuple((size for _, size in axes)) + (mesh.shape["con"],))
    torus_mesh = Mesh(devices, names + ("con",))
    in_specs = (P(names + ("con",), None), P(names, "con"), P())
    out_specs = P("con", names)
    return jax.shard_map(
        make_on_device(names),
        mesh=torus_mesh,
        in_specs=in_specs,
        out_specs=out_specs,
        check_vma=False,
    )
```

profile of v0, /device:TPU:1, one launch (start us, length us, event | category | flops | bytes accessed | tf_op | source)
XLA Modules:
  0.0 119.7 jit_solution(11476787945079464817)
XLA Ops:
  6.5 0.0 all-gather.4.cloned.1.call-start
  6.5 0.7 iota_compare_fusion
  7.3 0.1 broadcast_in_dim.20
  7.4 0.8 fusion.4
  8.2 4.8 %all-gather = bf16[2,2,9216]{2,1,0:T(2,128)(2,1)S(1)} all-gather(bf16[1,2,9216]{2,1,0:T(2,128)(2,1)S(1)} %fusion.4), channel_id=1, replica_groups=mesh['z'=8,'y'=4,'x'=4,'con'=2] {'con'}, dimensions={0}, use_global_device_ids=true | all-gather | bytes 110592 | tf_op jit(solution)/shard_map/all_gather | solution.py:32
  13.0 9.1 %all-gather.1 = bf16[4,4,4608]{2,1,0:T(4,128)(2,1)S(1)} all-gather(bf16[1,4,4608]{2,1,0:T(4,128)(2,1)S(1)} %dynamic-slice_bitcast_fusion), channel_id=1, replica_groups=mesh['z'=8,'y'=4,'x'=4,'con'=2] {'x'}, dimensions={0}, use_global_device_ids=true | all-gather | bytes 184320 | tf_op jit(solution)/shard_map/all_gather | solution.py:35
  22.2 10.8 %all_gather.14 = bf16[64,4608]{1,0:T(8,128)(2,1)} all-gather(bf16[16,4608]{1,0:T(8,128)(2,1)S(1)} %reshape.24), channel_id=1, replica_groups=mesh['z'=8,'y'=4,'x'=4,'con'=2] {'y'}, dimensions={0}, use_global_device_ids=true | all-gather | bytes 737280 | tf_op jit(solution)/shard_map/all_gather | solution.py:35
  33.0 0.0 all-gather.4.cloned.1.call-update
  33.0 66.2 %all-gather.4.cloned.1.call-done = bf16[512,4608]{1,0:T(8,128)(2,1)} async-done(((bf16[64,4608]{1,0:T(8,128)(2,1)}), bf16[512,4608]{1,0:T(8,128)(2,1)}) %all-gather.4.cloned.1.call-update) | async-done | bytes 4718608 | tf_op jit(solution)/shard_map/all_gather | solution.py:35
  99.2 6.0 %fusion = f32[256,1024]{1,0:T(8,128)S(1)} fusion(bf16[1024,4608]{1,0:T(8,128)(2,1)} %param.4, bf16[512,4608]{1,0:T(8,128)(2,1)} %all-gather.4.cloned.1.call-done, s32[]{:T(128)S(6)} %select_n.17), kind=kOutput, calls=%fused_computation | convolution fusion | flops 2415919104 | bytes 12845060 | tf_op jit(solution)/shard_map/dot_general | solution.py:20
  105.2 0.8 collective-permute-start
  105.9 6.0 %fusion.2 = f32[256,1024]{1,0:T(8,128)S(1)} fusion(bf16[1024,4608]{1,0:T(8,128)(2,1)} %param.4, bf16[512,4608]{1,0:T(8,128)(2,1)} %all-gather.4.cloned.1.call-done, s32[]{:T(128)S(6)} %select_n.16), kind=kOutput, calls=%fused_computation.2 | convolution fusion | flops 2415919104 | bytes 12845060 | tf_op jit(solution)/shard_map/dot_general | solution.py:20
  111.9 0.0 collective-permute-done
  111.9 1.0 add_convert_fusion
  (4 shorter events, 0.1 us)
Async XLA Ops:
  6.5 92.7 %all-gather.4.cloned.1.call-start = ((), (), s32[]{:S(2)}) async-start(), calls=%async_computation | async-start | bytes 5308416 | tf_op jit(solution)/shard_map/all_gather | solution.py:35
  105.2 6.7 %collective-permute-start = (f32[256,1024]{1,0:T(8,128)S(1)}, f32[256,1024]{1,0:T(8,128)S(1)}, u32[]{:S(2)}, u32[]{:S(2)}) collective-permute-start(f32[256,1024]{1,0:T(8,128)S(1)} %fusion), channel_id=1, source_target_pairs={{0,1},{1,0},{2,3},{3,2},{4,5},{5,4},{6,7},{7,6},{8,9},{9,8},{10,11... | collective-permute-start | bytes 3145736 | tf_op jit(solution)/shard_map/ppermute | solution.py:41
Sparse Core Ops, SparseCore 0:
  33.1 66.0 all-gather.3
where the time goes:
time: 120 us
  waiting for transfers between devices  66.2 us (55%)
  blocking collectives  24.7 us (21%)
  between operations  13.4 us (11%)
  matrix products  11.9 us (10%)
  other arithmetic  2.51 us (2%)
    all_gather x1, waiting for transfers between devices, on_device(): all_rows = lax.all_gather(all_rows, name, axis=0, tiled=True)  66.2 us
    all_gather x2, blocking collectives, on_device(): all_rows = lax.all_gather(all_rows, name, axis=0, tiled=True)  19.9 us
    dot_general x2, matrix products, contract(): lax.dot_general(amp_rows, integrals, (((1,), (1,)), ((), ())), preferred_...  11.9 us
    all_gather x1, blocking collectives, on_device(): chip_rows = lax.all_gather(masked, 'con', axis=0, tiled=True)  4.75 us
  transfers between devices with their start and end apart: 2, of which 1 were waited for; matrix products, arithmetic and copies ran while one was open for 5% of the time, Pallas kernels for 0%

commit v1 on v0

--- a/solution.py
+++ b/solution.py
@@ -32,7 +32,9 @@
         chip_rows = lax.all_gather(masked, "con", axis=0, tiled=True)
         all_rows = lax.dynamic_slice_in_dim(chip_rows, con * half, half, axis=1)
         for name in reversed(out_axes):
-            all_rows = lax.all_gather(all_rows, name, axis=0, tiled=True)
+            all_rows = jnp.concatenate(
+                lax.all_to_all(jnp.stack([all_rows] * lax.axis_size(name)), name, 0, 0), axis=0
+            )
         out_rows = all_rows.shape[0] // con_count
         other = 1 - con
         other_part = contract(

time: 120 us -> 158 us (1.32)
  waiting for transfers between devices: 66.2 us -> 104 us
  between operations: 13.4 us -> 0.06 us
  starting transfers between devices: 0.76 us -> 12.7 us
  local copies, waits for them, and re-layouts: 0.22 us -> 2.85 us
    all_to_all x0 -> x1, waiting for transfers between devices: none -> 104 us  [on_device(): lax.all_to_all(jnp.stack([all_rows] * lax.axis_size(name)), name, 0, 0)]
    all_gather x1 -> x0, waiting for transfers between devices: 66.2 us -> none  [on_device(): all_rows = lax.all_gather(all_rows, name, axis=0, tiled=True)]
    all_gather x2 -> x0, blocking collectives: 19.9 us -> none  [on_device(): all_rows = lax.all_gather(all_rows, name, axis=0, tiled=True)]
    all_to_all x0 -> x2, blocking collectives: none -> 19.1 us  [on_device(): lax.all_to_all(jnp.stack([all_rows] * lax.axis_size(name)), name, 0, 0)]
    all_to_all x0 -> x1, starting transfers between devices: none -> 8.19 us  [on_device(): lax.all_to_all(jnp.stack([all_rows] * lax.axis_size(name)), name, 0, 0)]
    ppermute x1, starting transfers between devices: 0.76 us -> 4.54 us  [on_device(): received = lax.ppermute(other_part, 'con', perm=[(0, 1), (1, 0)])]
    another operation x0 -> x4, local copies, waits for them, and re-layouts: none -> 2.67 us  [on_device(): jnp.stack([all_rows] * lax.axis_size(name))]
  transfers between devices with their start and end apart: 2 -> 2, of which waited for: 1 -> 1; matrix products, arithmetic and copies ran while one was open for 5% -> 4% of each run, Pallas kernels for 0% -> 0%
where the time goes in v1:
time: 158 us
  waiting for transfers between devices  104 us (66%)
  blocking collectives  23.9 us (15%)
  starting transfers between devices  12.7 us (8%)
  matrix products  11.9 us (8%)
  local copies, waits for them, and re-layouts  2.85 us (2%)
  other arithmetic  2.51 us (2%)
    all_to_all x1, waiting for transfers between devices, on_device(): lax.all_to_all(jnp.stack([all_rows] * lax.axis_size(name)), name, 0, 0)  104 us
    all_to_all x2, blocking collectives, on_device(): lax.all_to_all(jnp.stack([all_rows] * lax.axis_size(name)), name, 0, 0)  19.1 us
    dot_general x2, matrix products, contract(): lax.dot_general(amp_rows, integrals, (((1,), (1,)), ((), ())), preferred_...  11.9 us
    all_to_all x1, starting transfers between devices, on_device(): lax.all_to_all(jnp.stack([all_rows] * lax.axis_size(name)), name, 0, 0)  8.19 us
    all_gather x1, blocking collectives, on_device(): chip_rows = lax.all_gather(masked, 'con', axis=0, tiled=True)  4.75 us
    ppermute x1, starting transfers between devices, on_device(): received = lax.ppermute(other_part, 'con', perm=[(0, 1), (1, 0)])  4.54 us
  transfers between devices with their start and end apart: 2, of which 1 were waited for; matrix products, arithmetic and copies ran while one was open for 4% of the time, Pallas kernels for 0%

profile of v1, /device:TPU:1, one launch (start us, length us, event | category | flops | bytes accessed | tf_op | source)
XLA Modules:
  0.0 158.1 jit_solution(13865362904883242295)
XLA Ops:
  0.0 0.7 iota_compare_fusion
  0.7 0.1 broadcast_in_dim.20
  0.9 0.8 fusion.4
  1.7 4.8 %all-gather = bf16[2,2,9216]{2,1,0:T(2,128)(2,1)S(1)} all-gather(bf16[1,2,9216]{2,1,0:T(2,128)(2,1)S(1)} %fusion.4), channel_id=1, replica_groups=mesh['z'=8,'y'=4,'x'=4,'con'=2] {'con'}, dimensions={0}, use_global_device_ids=true | all-gather | bytes 110592 | tf_op jit(solution)/shard_map/all_gather | solution.py:32
  6.6 7.3 %all_to_all.15 = bf16[4,4,4608]{2,1,0:T(4,128)(2,1)S(1)} all-to-all(bf16[4,4,4608]{2,1,0:T(4,128)(2,1)S(1)} %stack.6), channel_id=1, replica_groups=mesh['z'=8,'y'=4,'x'=4,'con'=2] {'x'}, dimensions={0} | all-to-all | bytes 294912 | tf_op jit(solution)/shard_map/all_to_all | solution.py:36
  13.9 11.9 %all_to_all.16 = bf16[4,16,4608]{2,1,0:T(8,128)(2,1)S(1)} all-to-all(bf16[4,16,4608]{2,1,0:T(8,128)(2,1)S(1)} %stack.14), channel_id=1, replica_groups=mesh['z'=8,'y'=4,'x'=4,'con'=2] {'y'}, dimensions={0} | all-to-all | bytes 1179648 | tf_op jit(solution)/shard_map/all_to_all | solution.py:36
  25.8 2.6 %stack.15 = bf16[8,64,4608]{2,1,0:T(8,128)(2,1)} broadcast(bf16[64,4608]{1,0:T(8,128)(2,1)S(1)} %bitcast.6), dimensions={1,2} | broadcast | bytes 5308416 | tf_op jit(solution)/shard_map/stack | solution.py:36
  28.3 8.2 %all-to-all-start.2 = ((bf16[8,64,4608]{2,1,0:T(8,128)(2,1)}), bf16[8,64,4608]{2,1,0:T(8,128)(2,1)}, u32[]{:S(2)}, u32[]{:S(2)}) async-start(bf16[8,64,4608]{2,1,0:T(8,128)(2,1)} %stack.15), calls=%async_computation.2 | async-start | bytes 9437184 | tf_op jit(solution)/shard_map/all_to_all | solution.py:36
  36.5 104.1 %all-to-all-done.2 = bf16[8,64,4608]{2,1,0:T(8,128)(2,1)} async-done(((bf16[8,64,4608]{2,1,0:T(8,128)(2,1)}), bf16[8,64,4608]{2,1,0:T(8,128)(2,1)}, u32[]{:S(2)}, u32[]{:S(2)}) %all-to-all-start.2) | async-done | bytes 4718624 | tf_op jit(solution)/shard_map/all_to_all | solution.py:36
  140.6 6.0 %fusion = f32[256,1024]{1,0:T(8,128)S(1)} fusion(bf16[1024,4608]{1,0:T(8,128)(2,1)} %param.4, bf16[512,4608]{1,0:T(8,128)(2,1)} %bitcast.2, s32[]{:T(128)S(6)} %select_n.17), kind=kOutput, calls=%fused_computation | convolution fusion | flops 2415919104 | bytes 12845060 | tf_op jit(solution)/shard_map/dot_general | solution.py:20
  146.6 4.5 %collective-permute-start = (f32[256,1024]{1,0:T(8,128)S(1)}, f32[256,1024]{1,0:T(8,128)S(1)}, u32[]{:S(2)}, u32[]{:S(2)}) collective-permute-start(f32[256,1024]{1,0:T(8,128)S(1)} %fusion), channel_id=1, source_target_pairs={{0,1},{1,0},{2,3},{3,2},{4,5},{5,4},{6,7},{7,6},{8,9},{9,8},{10,11... | collective-permute-start | bytes 3145736 | tf_op jit(solution)/shard_map/ppermute | solution.py:43
  151.2 6.0 %fusion.2 = f32[256,1024]{1,0:T(8,128)S(1)} fusion(bf16[1024,4608]{1,0:T(8,128)(2,1)} %param.4, bf16[512,4608]{1,0:T(8,128)(2,1)} %bitcast.2, s32[]{:T(128)S(6)} %select_n.16), kind=kOutput, calls=%fused_computation.2 | convolution fusion | flops 2415919104 | bytes 12845060 | tf_op jit(solution)/shard_map/dot_general | solution.py:20
  157.1 0.0 collective-permute-done
  157.1 1.0 add_convert_fusion
  (6 shorter events, 0.2 us)
Async XLA Ops:
  28.3 112.3 %all-to-all-start.2 = ((bf16[8,64,4608]{2,1,0:T(8,128)(2,1)}), bf16[8,64,4608]{2,1,0:T(8,128)(2,1)}, u32[]{:S(2)}, u32[]{:S(2)}) async-start(bf16[8,64,4608]{2,1,0:T(8,128)(2,1)} %stack.15), calls=%async_computation.2 | async-start | bytes 9437184 | tf_op jit(solution)/shard_map/all_to_all | solution.py:36
  146.6 10.5 %collective-permute-start = (f32[256,1024]{1,0:T(8,128)S(1)}, f32[256,1024]{1,0:T(8,128)S(1)}, u32[]{:S(2)}, u32[]{:S(2)}) collective-permute-start(f32[256,1024]{1,0:T(8,128)S(1)} %fusion), channel_id=1, source_target_pairs={{0,1},{1,0},{2,3},{3,2},{4,5},{5,4},{6,7},{7,6},{8,9},{9,8},{10,11... | collective-permute-start | bytes 3145736 | tf_op jit(solution)/shard_map/ppermute | solution.py:43
